TPU v7x, 256 devices: a whole 4x4x8 slice. The times are simulated.
256 devices in a mesh: rows: 8 (over x, core), cols: 32 (over y, z).
Axes of the slice: x: 4, y: 4, z: 8, core: 2. Of those that a mesh axis runs over, the one named last changes fastest.
Arguments:
- features: bfloat16 [256, 4096, 1536], P('rows', 'cols'), may hold values from -6 to 6
- projection: bfloat16 [1536, 128], replicated, may hold values from -0.4375 to 0.4375
- prev_dist: float32 [256, 4096], P('rows', 'cols'), may hold values from 0.5 to 3
- valid: int32 [256, 4096], P('rows', 'cols'), may hold values 0 or 1
- pick_owner: int32 [512], replicated, may hold values from 0 to 255, as said below
- pick_slot: int32 [512], replicated, may hold values from 0 to 4095, as said below
Outputs:
- min_dist: float32 [256, 4096], P('rows', 'cols')
Inputs may be any that keep to these rules, and one draw needn't show every extreme that they name: `pick_owner`: no two picks name the same patch; picks fall on devices at random. `pick_slot`: see pick_owner.
All inputs are finite; a program needn't handle non-finite values. No bound on the sum of `valid` on one device may be relied on, other than what follows from the above.
Results may differ from a plain program's by a relative error of at most 0.0003.
Values may be sent and summed in bfloat16 or wider, within the bound.
A program may use at most 128 MiB of HBM per device.

v0:
```python
import jax
import jax.numpy as jnp
from jax import lax
from jax.sharding import PartitionSpec as P

D_PROJ = 128


def padded_2(block, sides, width):
    for axis, dim in sides:
        count = lax.axis_size(axis)
        forward = [(i, i + 1) for i in range(count - 1)]
        backward = [(target, source) for source, target in forward]
        low = lax.ppermute(
            lax.slice_in_dim(block, block.shape[dim] - width, None, axis=dim), axis, forward
        )
        high = lax.ppermute(lax.slice_in_dim(block, 0, width, axis=dim), axis, backward)
        block = jnp.concatenate([low, block, high], axis=dim)
    return block


def window_sum(padded, rows_dev, cols_dev):
    total = jnp.zeros((rows_dev, cols_dev, padded.shape[2]), jnp.float32)
    for row_off in range(3):
        for col_off in range(3):
            total = total + padded[
                row_off : row_off + rows_dev, col_off : col_off + cols_dev
            ].astype(jnp.float32)
    return total / 9.0


def shards(features, projection, prev_dist, valid, pick_owner, pick_slot):
    rows_dev, cols_dev, channels = features.shape
    proj_full = projection.astype(jnp.float32)
    own_index = lax.axis_index("rows") * lax.axis_size("cols") + lax.axis_index("cols")
    owned = pick_owner == own_index
    padded = padded_2(features, (("rows", 0), ("cols", 1)), 1)
    pooled = window_sum(padded, rows_dev, cols_dev).reshape(rows_dev * cols_dev, channels)
    projected = jnp.dot(pooled, proj_full, precision=lax.Precision.HIGHEST)
    local_rows = jnp.where(owned[:, None], projected[pick_slot], jnp.float32(0.0))
    pick_rows = lax.psum(local_rows, ("rows", "cols"))
    pick_sq = jnp.sum(pick_rows * pick_rows, axis=1)
    own_sq = jnp.sum(projected * projected, axis=1)
    inner_prod = jnp.dot(projected, pick_rows.T, precision=lax.Precision.HIGHEST)
    scaled_gap = (own_sq[:, None] + pick_sq[None, :] - 2.0 * inner_prod) / D_PROJ
    nearest = jnp.min(scaled_gap, axis=1).reshape(rows_dev, cols_dev)
    return jnp.where(valid == 1, jnp.minimum(prev_dist, nearest), jnp.float32(0.0))


def solution(mesh):
    return jax.shard_map(
        shards,
        mesh=mesh,
        in_specs=(P("rows", "cols", None), P(), P("rows", "cols"), P("rows", "cols"), P(), P()),
        out_specs=P("rows", "cols"),
        check_vma=False,
    )
```

profile of v0, /device:TPU:2, one launch (start us, length us, event | category | flops | bytes accessed | tf_op | source)
XLA Modules:
  0.0 382.1 jit_solution(17740806826330092399)
XLA Ops:
  6.5 1.2 fusion.6
  7.8 1.9 collective-permute-start
  9.7 3.6 collective-permute-start.1
  13.3 0.7 broadcast_compare_fusion
  14.0 0.7 compare_select_fusion
  14.7 2.1 collective-permute-done
  16.9 6.7 %constant_dynamic-update-slice_fusion.1 = bf16[34,128,1536]{2,1,0:T(8,128)(2,1)S(1)} fusion(bf16[34,128,1536]{2,1,0:T(8,128)(2,1)S(1)} %constant_dynamic-update-slice_fusion.2, bf16[32,128,1536]{2,1,0:T(8,128)(2,1)} %param.6), kind=kLoop, calls=%fused_computation.25 | loop fusion | bytes 25165824
  23.6 4.8 %copy-done.1 = bf16[34,128,1536]{2,1,0:T(8,128)(2,1)} copy-done((bf16[34,128,1536]{2,1,0:T(8,128)(2,1)}, bf16[34,128,1536]{2,1,0:T(8,128)(2,1)S(1)}, u32[]{:S(2)}) %copy-start.1) | copy-done | bytes 13369368
  28.5 0.3 fusion.5
  28.8 3.8 %collective-permute-start.2 = (bf16[34,1,1536]{2,0,1:T(8,128)(2,1)S(1)}, bf16[34,1,1536]{2,0,1:T(8,128)(2,1)S(1)}, u32[]{:S(2)}, u32[]{:S(2)}) collective-permute-start(bf16[34,1,1536]{2,0,1:T(8,128)(2,1)S(1)} %copy.15), channel_id=1, source_target_pairs={{0,1},{1,2},{2,3},{3,4},{4,5},{5,6},{6,7},{7,8},{8,9},{9,10},{10,1... | collective-permute-start | bytes 313352 | tf_op jit(solution)/shard_map/ppermute | solution.py:14
  32.7 1.3 collective-permute-start.3
  34.0 1.1 collective-permute-done.2
  35.1 0.2 copy.16
  35.2 4.2 %collective-permute-done.3 = bf16[34,1,1536]{2,0,1:T(8,128)(2,1)S(1)} collective-permute-done((bf16[34,1,1536]{2,0,1:T(8,128)(2,1)S(1)}, bf16[34,1,1536]{2,0,1:T(8,128)(2,1)S(1)}, u32[]{:S(2)}, u32[]{:S(2)}) %collective-permute-start.3) | collective-permute-done | bytes 104480 | tf_op jit(solution)/shard_map/ppermute | solution.py:17
  39.5 0.2 copy.18
  39.6 47.2 %add_multiply_fusion = f32[32,128,1536]{2,1,0:T(8,128)} fusion(bf16[32,128,1536]{2,1,0:T(8,128)(2,1)} %param.6, bf16[34,128,1536]{2,1,0:T(8,128)(2,1)} %copy-done.1, bf16[34,1,1536]{2,1,0:T(2,128)(2,1)S(1)} %copy.18, bf16[34,1,1536]{2,1,0:T(2,128)(2,1)S(1)} %copy.16, bf16[1,128,1536]{2,1,0:T(8,128)(2,1)S(1)} %collective-permute-done.1, ...), kind=kLoop, calls=%fused_computation.1 | loop fusion | flops 264241152 | bytes 52113408 | tf_op jit(solution)/shard_map/div | solution.py:29
  86.9 18.7 %multiply_reduce_fusion.1 = (f32[4096]{0:T(1024)S(1)}, f32[4096,128]{0,1:T(8,128)S(1)}) fusion(f32[4096,1536]{1,0:T(8,128)} %bitcast.9, bf16[1536,128]{1,0:T(8,128)(2,1)S(1)} %copy-done), kind=kOutput, calls=%fused_computation.19 | convolution fusion | flops 9664720896 | bytes 27672576 | tf_op jit(solution)/shard_map/dot_general | solution.py:39
  105.6 1.9 copy.19
  107.5 2.6 gather_fusion
  110.1 0.8 broadcast_select_fusion
  111.0 253.3 %all-reduce.2.cloned.1.call-done = f32[512,128]{1,0:T(8,128)} async-done(((f32[512,128]{1,0:T(8,128)}), f32[512,128]{1,0:T(8,128)}) %all-reduce.2.cloned.1.call-update) | async-done | bytes 262160 | tf_op jit(solution)/shard_map/psum | solution.py:41
  364.3 1.1 multiply_reduce_fusion.2
  365.4 9.2 %multiply_reduce_fusion = f32[4096]{0:T(1024)S(1)} fusion(f32[4096,128]{0,1:T(8,128)S(1)} %get-tuple-element.10, f32[512,128]{1,0:T(8,128)} %all-reduce.2.cloned.1.call-done, f32[512]{0:T(512)S(1)} %multiply_reduce_fusion.2, f32[4096]{0:T(1024)S(1)} %get-tuple-element.9), kind=kOutput, calls=%fused_computation.18 | convolution fusion | flops 3231707136 | bytes 2394112 | tf_op jit(solution)/shard_map/dot_general | solution.py:44
  374.7 0.6 fusion.4
  (15 shorter events, 0.1 us)
Async XLA Ops:
  6.5 80.3 %copy-start = (bf16[1536,128]{1,0:T(8,128)(2,1)S(1)}, bf16[1536,128]{1,0:T(8,128)(2,1)}, u32[]{:S(2)}) copy-start(bf16[1536,128]{1,0:T(8,128)(2,1)} %param.7) | copy-start | bytes 1179652
  6.5 357.8 %all-reduce.2.cloned.1.call-start = ((), (), s32[]{:S(2)}) async-start(), calls=%async_computation | async-start | bytes 524288 | tf_op jit(solution)/shard_map/psum | solution.py:41
  7.8 9.1 %collective-permute-start = (bf16[1,128,1536]{2,1,0:T(8,128)(2,1)S(1)}, bf16[1,128,1536]{2,1,0:T(8,128)(2,1)S(1)}, u32[]{:S(2)}, u32[]{:S(2)}) collective-permute-start(bf16[1,128,1536]{2,1,0:T(8,128)(2,1)S(1)} %get-tuple-element.8), channel_id=1, source_target_pairs={{0,32},{32,64},{64,96},{96,128},{128,160},{160,192},{192,224},{1,3... | collective-permute-start | bytes 1179656 | tf_op jit(solution)/shard_map/ppermute | solution.py:14
  9.7 13.9 %collective-permute-start.1 = (bf16[1,128,1536]{2,1,0:T(8,128)(2,1)S(1)}, bf16[1,128,1536]{2,1,0:T(8,128)(2,1)S(1)}, u32[]{:S(2)}, u32[]{:S(2)}) collective-permute-start(bf16[1,128,1536]{2,1,0:T(8,128)(2,1)S(1)} %get-tuple-element.7), channel_id=1, source_target_pairs={{32,0},{64,32},{96,64},{128,96},{160,128},{192,160},{224,192},{33,... | collective-permute-start | bytes 1179656 | tf_op jit(solution)/shard_map/ppermute | solution.py:17
  23.6 4.8 %copy-start.1 = (bf16[34,128,1536]{2,1,0:T(8,128)(2,1)}, bf16[34,128,1536]{2,1,0:T(8,128)(2,1)S(1)}, u32[]{:S(2)}) copy-start(bf16[34,128,1536]{2,1,0:T(8,128)(2,1)S(1)} %constant_dynamic-update-slice_fusion) | copy-start | bytes 40108036
  28.8 6.3 %collective-permute-start.2 = (bf16[34,1,1536]{2,0,1:T(8,128)(2,1)S(1)}, bf16[34,1,1536]{2,0,1:T(8,128)(2,1)S(1)}, u32[]{:S(2)}, u32[]{:S(2)}) collective-permute-start(bf16[34,1,1536]{2,0,1:T(8,128)(2,1)S(1)} %copy.15), channel_id=1, source_target_pairs={{0,1},{1,2},{2,3},{3,4},{4,5},{5,6},{6,7},{7,8},{8,9},{9,10},{10,1... | collective-permute-start | bytes 313352 | tf_op jit(solution)/shard_map/ppermute | solution.py:14
  32.7 6.8 %collective-permute-start.3 = (bf16[34,1,1536]{2,0,1:T(8,128)(2,1)S(1)}, bf16[34,1,1536]{2,0,1:T(8,128)(2,1)S(1)}, u32[]{:S(2)}, u32[]{:S(2)}) collective-permute-start(bf16[34,1,1536]{2,0,1:T(8,128)(2,1)S(1)} %copy.17), channel_id=1, source_target_pairs={{1,0},{2,1},{3,2},{4,3},{5,4},{6,5},{7,6},{8,7},{9,8},{10,9},{11,1... | collective-permute-start | bytes 313352 | tf_op jit(solution)/shard_map/ppermute | solution.py:17
  105.6 269.0 %copy-start.2 = (f32[32,128]{1,0:T(8,128)S(1)}, f32[32,128]{1,0:T(8,128)}, u32[]{:S(2)}) copy-start(f32[32,128]{1,0:T(8,128)} %param.8) | copy-start | bytes 49156
  105.6 269.0 %copy-start.3 = (s32[32,128]{1,0:T(8,128)S(1)}, s32[32,128]{1,0:T(8,128)}, u32[]{:S(2)}) copy-start(s32[32,128]{1,0:T(8,128)} %param.9) | copy-start | bytes 49156
Sparse Core Ops, SparseCore 0:
  111.1 253.1 all-reduce.1
where the time goes:
time: 382 us
  waiting for transfers between devices  261 us (68%)
  other arithmetic  51.2 us (13%)
  matrix products  27.9 us (7%)
  local copies, waits for them, and re-layouts  18 us (5%)
  between operations  13.6 us (4%)
  starting transfers between devices  10.7 us (3%)
    psum x1, waiting for transfers between devices, shards(): pick_rows = lax.psum(local_rows, ('rows', 'cols'))  253 us
    div x1, other arithmetic, window_sum(): return total / 9.0  47.2 us
    dot_general x1, matrix products, shards(): projected = jnp.dot(pooled, proj_full, precision=lax.Precision.HIGHEST)  18.7 us
    unnamed x10, local copies, waits for them, and re-layouts  11.6 us
    dot_general x1, matrix products, shards(): jnp.dot(projected, pick_rows.T, precision=lax.Precision.HIGHEST)  9.21 us
  transfers between devices with their start and end apart: 5, of which 4 were waited for; matrix products, arithmetic and copies ran while one was open for 2% of the time, Pallas kernels for 0%

commit v1 on v0

--- a/solution.py
+++ b/solution.py
@@ -38,7 +38,7 @@
     pooled = window_sum(padded, rows_dev, cols_dev).reshape(rows_dev * cols_dev, channels)
     projected = jnp.dot(pooled, proj_full, precision=lax.Precision.HIGHEST)
     local_rows = jnp.where(owned[:, None], projected[pick_slot], jnp.float32(0.0))
-    pick_rows = lax.psum(local_rows, ("rows", "cols"))
+    pick_rows = lax.psum(lax.psum(local_rows, "cols"), "rows")
     pick_sq = jnp.sum(pick_rows * pick_rows, axis=1)
     own_sq = jnp.sum(projected * projected, axis=1)
     inner_prod = jnp.dot(projected, pick_rows.T, precision=lax.Precision.HIGHEST)

time: 382 us -> 340 us (0.89)
  waiting for transfers between devices: 261 us -> 216 us
    psum x1 -> x2, waiting for transfers between devices: 253 us -> 209 us  [shards(): pick_rows = lax.psum(lax.psum(local_rows, 'cols'), 'rows')]
  transfers between devices with their start and end apart: 5 -> 6, of which waited for: 4 -> 5; matrix products, arithmetic and copies ran while one was open for 2% -> 2% of each run, Pallas kernels for 0% -> 0%
where the time goes in v1:
time: 340 us; the launch traced here: 338 us
  waiting for transfers between devices  216 us (64%)
  other arithmetic  51.2 us (15%)
  matrix products  27.8 us (8%)
  local copies, waits for them, and re-layouts  18 us (5%)
  between operations  13.6 us (4%)
  starting transfers between devices  10.9 us (3%)
    psum x2, waiting for transfers between devices, shards(): pick_rows = lax.psum(lax.psum(local_rows, 'cols'), 'rows')  209 us
    div x1, other arithmetic, window_sum(): return total / 9.0  47.2 us
    dot_general x1, matrix products, shards(): projected = jnp.dot(pooled, proj_full, precision=lax.Precision.HIGHEST)  18.7 us
    unnamed x10, local copies, waits for them, and re-layouts  11.6 us
    dot_general x1, matrix products, shards(): jnp.dot(projected, pick_rows.T, precision=lax.Precision.HIGHEST)  9.02 us
  transfers between devices with their start and end apart: 6, of which 5 were waited for; matrix products, arithmetic and copies ran while one was open for 2% of the time, Pallas kernels for 0%

profile of v1, /device:TPU:2, one launch (start us, length us, event | category | flops | bytes accessed | tf_op | source)
XLA Modules:
  0.0 337.8 jit_solution(7706667509816880788)
XLA Ops:
  6.5 1.2 fusion.6
  7.8 1.9 collective-permute-start
  9.7 3.6 %collective-permute-start.1 = (bf16[1,128,1536]{2,1,0:T(8,128)(2,1)S(1)}, bf16[1,128,1536]{2,1,0:T(8,128)(2,1)S(1)}, u32[]{:S(2)}, u32[]{:S(2)}) collective-permute-start(bf16[1,128,1536]{2,1,0:T(8,128)(2,1)S(1)} %get-tuple-element.7), channel_id=1, source_target_pairs={{32,0},{64,32},{96,64},{128,96},{160,128},{192,160},{224,192},{33,... | collective-permute-start | bytes 1179656 | tf_op jit(solution)/shard_map/ppermute | solution.py:17
  13.3 0.7 broadcast_compare_fusion
  14.0 0.7 compare_select_fusion
  14.7 2.1 collective-permute-done
  16.9 6.7 %constant_dynamic-update-slice_fusion.1 = bf16[34,128,1536]{2,1,0:T(8,128)(2,1)S(1)} fusion(bf16[34,128,1536]{2,1,0:T(8,128)(2,1)S(1)} %constant_dynamic-update-slice_fusion.2, bf16[32,128,1536]{2,1,0:T(8,128)(2,1)} %param.6), kind=kLoop, calls=%fused_computation.25 | loop fusion | bytes 25165824
  23.6 4.8 %copy-done.1 = bf16[34,128,1536]{2,1,0:T(8,128)(2,1)} copy-done((bf16[34,128,1536]{2,1,0:T(8,128)(2,1)}, bf16[34,128,1536]{2,1,0:T(8,128)(2,1)S(1)}, u32[]{:S(2)}) %copy-start.1) | copy-done | bytes 13369368
  28.5 0.3 fusion.5
  28.8 3.8 %collective-permute-start.2 = (bf16[34,1,1536]{2,0,1:T(8,128)(2,1)S(1)}, bf16[34,1,1536]{2,0,1:T(8,128)(2,1)S(1)}, u32[]{:S(2)}, u32[]{:S(2)}) collective-permute-start(bf16[34,1,1536]{2,0,1:T(8,128)(2,1)S(1)} %copy.15), channel_id=1, source_target_pairs={{0,1},{1,2},{2,3},{3,4},{4,5},{5,6},{6,7},{7,8},{8,9},{9,10},{10,1... | collective-permute-start | bytes 313352 | tf_op jit(solution)/shard_map/ppermute | solution.py:14
  32.7 1.3 collective-permute-start.3
  34.0 1.1 collective-permute-done.2
  35.2 4.2 %collective-permute-done.3 = bf16[34,1,1536]{2,0,1:T(8,128)(2,1)S(1)} collective-permute-done((bf16[34,1,1536]{2,0,1:T(8,128)(2,1)S(1)}, bf16[34,1,1536]{2,0,1:T(8,128)(2,1)S(1)}, u32[]{:S(2)}, u32[]{:S(2)}) %collective-permute-start.3) | collective-permute-done | bytes 104480 | tf_op jit(solution)/shard_map/ppermute | solution.py:17
  39.6 47.2 %add_multiply_fusion = f32[32,128,1536]{2,1,0:T(8,128)} fusion(bf16[32,128,1536]{2,1,0:T(8,128)(2,1)} %param.6, bf16[34,128,1536]{2,1,0:T(8,128)(2,1)} %copy-done.1, bf16[34,1,1536]{2,1,0:T(2,128)(2,1)S(1)} %copy.18, bf16[34,1,1536]{2,1,0:T(2,128)(2,1)S(1)} %copy.16, bf16[1,128,1536]{2,1,0:T(8,128)(2,1)S(1)} %collective-permute-done.1, ...), kind=kLoop, calls=%fused_computation.1 | loop fusion | flops 264241152 | bytes 52113408 | tf_op jit(solution)/shard_map/div | solution.py:29
  86.9 18.7 %multiply_reduce_fusion.1 = (f32[4096]{0:T(1024)S(1)}, f32[4096,128]{0,1:T(8,128)S(1)}) fusion(f32[4096,1536]{1,0:T(8,128)} %bitcast.9, bf16[1536,128]{1,0:T(8,128)(2,1)S(1)} %copy-done), kind=kOutput, calls=%fused_computation.19 | convolution fusion | flops 9664720896 | bytes 27672576 | tf_op jit(solution)/shard_map/dot_general | solution.py:39
  105.6 1.9 copy.19
  107.5 2.6 gather_fusion
  110.1 0.8 broadcast_select_fusion
  111.0 0.2 all-reduce.5.cloned.1.call-start
  111.2 146.9 %all-reduce.3.cloned.1.call-done = f32[512,128]{1,0:T(8,128)} async-done(((f32[512,128]{1,0:T(8,128)}), f32[512,128]{1,0:T(8,128)}) %all-reduce.3.cloned.1.call-update) | async-done | bytes 262160 | tf_op jit(solution)/shard_map/psum | solution.py:41
  258.1 62.0 %all-reduce.5.cloned.1.call-done = f32[512,128]{1,0:T(8,128)} async-done(((f32[512,128]{1,0:T(8,128)}), f32[512,128]{1,0:T(8,128)}) %all-reduce.5.cloned.1.call-update) | async-done | bytes 262160 | tf_op jit(solution)/shard_map/psum | solution.py:41
  320.2 1.1 multiply_reduce_fusion.2
  321.3 9.0 %multiply_reduce_fusion = f32[4096]{0:T(1024)S(1)} fusion(f32[4096,128]{0,1:T(8,128)S(1)} %get-tuple-element.10, f32[512,128]{1,0:T(8,128)} %all-reduce.5.cloned.1.call-done, f32[512]{0:T(512)S(1)} %multiply_reduce_fusion.2, f32[4096]{0:T(1024)S(1)} %get-tuple-element.9), kind=kOutput, calls=%fused_computation.18 | convolution fusion | flops 3231707136 | bytes 2394112 | tf_op jit(solution)/shard_map/dot_general | solution.py:44
  330.3 0.6 fusion.4
  (18 shorter events, 0.5 us)
Async XLA Ops:
  6.5 80.3 %copy-start = (bf16[1536,128]{1,0:T(8,128)(2,1)S(1)}, bf16[1536,128]{1,0:T(8,128)(2,1)}, u32[]{:S(2)}) copy-start(bf16[1536,128]{1,0:T(8,128)(2,1)} %param.7) | copy-start | bytes 1179652
  6.5 251.6 %all-reduce.3.cloned.1.call-start = ((), (), s32[]{:S(2)}) async-start(), calls=%async_computation | async-start | bytes 524288 | tf_op jit(solution)/shard_map/psum | solution.py:41
  7.8 9.1 %collective-permute-start = (bf16[1,128,1536]{2,1,0:T(8,128)(2,1)S(1)}, bf16[1,128,1536]{2,1,0:T(8,128)(2,1)S(1)}, u32[]{:S(2)}, u32[]{:S(2)}) collective-permute-start(bf16[1,128,1536]{2,1,0:T(8,128)(2,1)S(1)} %get-tuple-element.8), channel_id=1, source_target_pairs={{0,32},{32,64},{64,96},{96,128},{128,160},{160,192},{192,224},{1,3... | collective-permute-start | bytes 1179656 | tf_op jit(solution)/shard_map/ppermute | solution.py:14
  9.7 13.9 %collective-permute-start.1 = (bf16[1,128,1536]{2,1,0:T(8,128)(2,1)S(1)}, bf16[1,128,1536]{2,1,0:T(8,128)(2,1)S(1)}, u32[]{:S(2)}, u32[]{:S(2)}) collective-permute-start(bf16[1,128,1536]{2,1,0:T(8,128)(2,1)S(1)} %get-tuple-element.7), channel_id=1, source_target_pairs={{32,0},{64,32},{96,64},{128,96},{160,128},{192,160},{224,192},{33,... | collective-permute-start | bytes 1179656 | tf_op jit(solution)/shard_map/ppermute | solution.py:17
  23.6 4.8 %copy-start.1 = (bf16[34,128,1536]{2,1,0:T(8,128)(2,1)}, bf16[34,128,1536]{2,1,0:T(8,128)(2,1)S(1)}, u32[]{:S(2)}) copy-start(bf16[34,128,1536]{2,1,0:T(8,128)(2,1)S(1)} %constant_dynamic-update-slice_fusion) | copy-start | bytes 40108036
  28.8 6.3 %collective-permute-start.2 = (bf16[34,1,1536]{2,0,1:T(8,128)(2,1)S(1)}, bf16[34,1,1536]{2,0,1:T(8,128)(2,1)S(1)}, u32[]{:S(2)}, u32[]{:S(2)}) collective-permute-start(bf16[34,1,1536]{2,0,1:T(8,128)(2,1)S(1)} %copy.15), channel_id=1, source_target_pairs={{0,1},{1,2},{2,3},{3,4},{4,5},{5,6},{6,7},{7,8},{8,9},{9,10},{10,1... | collective-permute-start | bytes 313352 | tf_op jit(solution)/shard_map/ppermute | solution.py:14
  32.7 6.8 %collective-permute-start.3 = (bf16[34,1,1536]{2,0,1:T(8,128)(2,1)S(1)}, bf16[34,1,1536]{2,0,1:T(8,128)(2,1)S(1)}, u32[]{:S(2)}, u32[]{:S(2)}) collective-permute-start(bf16[34,1,1536]{2,0,1:T(8,128)(2,1)S(1)} %copy.17), channel_id=1, source_target_pairs={{1,0},{2,1},{3,2},{4,3},{5,4},{6,5},{7,6},{8,7},{9,8},{10,9},{11,1... | collective-permute-start | bytes 313352 | tf_op jit(solution)/shard_map/ppermute | solution.py:17
  105.6 224.7 %copy-start.2 = (f32[32,128]{1,0:T(8,128)S(1)}, f32[32,128]{1,0:T(8,128)}, u32[]{:S(2)}) copy-start(f32[32,128]{1,0:T(8,128)} %param.8) | copy-start | bytes 49156
  105.6 224.7 %copy-start.3 = (s32[32,128]{1,0:T(8,128)S(1)}, s32[32,128]{1,0:T(8,128)}, u32[]{:S(2)}) copy-start(s32[32,128]{1,0:T(8,128)} %param.9) | copy-start | bytes 49156
  111.0 209.2 %all-reduce.5.cloned.1.call-start = ((), (), s32[]{:S(2)}) async-start(), calls=%async_computation.1 | async-start | bytes 524288 | tf_op jit(solution)/shard_map/psum | solution.py:41
Sparse Core Ops, SparseCore 0:
  111.1 146.9 all-reduce.2
  260.4 59.6 all-reduce.4
